TPU v7x, 256 devices: a whole 4x4x8 slice. The times are simulated.
256 devices in a mesh: grp: 8 (over x, core), dev: 32 (over y, z).
Axes of the slice: x: 4, y: 4, z: 8, core: 2. Of those that a mesh axis runs over, the one named last changes fastest.
Arguments:
- queries: bfloat16 [65536, 768], P(('grp', 'dev')), may hold values from -1.796875 to 1.796875
- query_slots: int32 [65536], P('grp'), may hold values from 0 to 8191, as said below
- w_res: bfloat16 [768, 768], replicated, may hold values from -0.21875 to 0.21875
- labels: bfloat16 [5120, 128, 768], P(('grp', 'dev')), may hold values from -0.71875 to 0.71875
- blocks: int32 [512, 12], P('grp'), may hold values from 0 to 5119, as said below
- positives: int32 [65536, 4], P(('grp', 'dev')), may hold values from 0 to 655359, as said below
Outputs:
- query_loss: float32 [65536], P(('grp', 'dev'))
- query_grad: bfloat16 [65536, 768], P(('grp', 'dev'))
- label_grad: bfloat16 [5120, 128, 768], P(('grp', 'dev'))
- residual_grad: bfloat16 [768, 768], replicated
Inputs may be any that keep to these rules, and one draw needn't show every extreme that they name: `query_slots`: the rows of one grp index (rows g * 256 * 32 onward) hold a permutation of 0 to 8191; a place // 256 is the dev index that owns the query's cluster, and the 256 rows of every device send exactly 8 queries to each owner. Row c lists 12 different blocks, all held by devices of the same grp index as the cluster's owner (device c // 2). The 2 clusters of one device list at most 16 distinct blocks, of which at most 1 are held by any one device; for every device's clusters some holder reaches 1. `positives`: the 4 labels of row r are different and lie in 4 different blocks listed for cluster r // 128.
All inputs are finite; a program needn't handle non-finite values.
Results may differ from a plain program's by a relative error of at most 0.0047.
The roundings to bfloat16 on the way count: a program that leaves them out, or rounds other values in their place, can miss the bound.
Values may be sent and summed in bfloat16 or wider, within the bound.
No kernel may reach another device: no remote copies, remote signals or barrier semaphores. Data moves between devices by JAX's collectives and lax.ppermute only.
A program may use at most 128 MiB of HBM per device.

v0:
```python
from functools import partial
import jax
import jax.numpy as jnp
from jax import lax
from jax.sharding import PartitionSpec as P

BLK = 128
CSIZE = 128
SHORT = 12
NPOS = 4
POOL = 16
BLK_DEV = 20


def activate(values):
    return jax.nn.gelu(values, approximate=True)


def activate_slope(values):
    return jax.vjp(activate, values)[1](jnp.ones_like(values))[0]


def request_plan(listed, owner_base, peer_count, per_owner):
    owners = listed // BLK_DEV - owner_base
    within = listed % BLK_DEV
    positions = jnp.arange(listed.shape[0], dtype=jnp.int32)
    earlier = positions[None, :] < positions[:, None]
    same_block = listed[:, None] == listed[None, :]
    leading = jnp.logical_not(jnp.any(same_block & earlier, axis=1))
    first_seen = jnp.argmax(same_block, axis=1)
    same_owner = owners[:, None] == owners[None, :]
    ranking = jnp.sum(same_owner & earlier & leading[None, :], axis=1)
    own_place = owners * per_owner + ranking
    placed = own_place[first_seen]
    target = jnp.where(leading, own_place, peer_count * per_owner)
    request_table = (
        jnp.full((peer_count * per_owner,), -1, jnp.int32).at[target].set(within, mode="drop")
    )
    return (placed, request_table.reshape(peer_count, per_owner))


def local(queries, query_slots, w_res, labels, blocks, positives):
    peer_count = lax.axis_size("dev")
    groups = lax.axis_size("grp")
    own_index = lax.axis_index("dev")
    group_index = lax.axis_index("grp")
    rows_dev = queries.shape[0]
    feature_width = queries.shape[1]
    per_peer = rows_dev // peer_count
    clusters_dev = rows_dev // CSIZE
    per_owner = (POOL + peer_count - 1) // peer_count
    slots_total = peer_count * per_owner
    own_slots = lax.dynamic_slice_in_dim(query_slots, own_index * rows_dev, rows_dev)
    outbound = jnp.argsort(own_slots // rows_dev, stable=True)
    slot_grid = query_slots.reshape(peer_count, rows_dev)
    grid_order = jnp.argsort(slot_grid // rows_dev, axis=1, stable=True)
    grid_sorted = jnp.take_along_axis(slot_grid, grid_order, axis=1)
    incoming = (
        lax.dynamic_slice_in_dim(grid_sorted, own_index * per_peer, per_peer, 1).reshape(rows_dev)
        - own_index * rows_dev
    )
    arrange = jnp.argsort(incoming)
    pre_act = jnp.dot(queries, w_res, preferred_element_type=jnp.float32)
    payload = (queries.astype(jnp.float32) + activate(pre_act)).astype(jnp.bfloat16)
    arrived = lax.all_to_all(
        payload[outbound].reshape(peer_count, per_peer, feature_width),
        "dev",
        split_axis=0,
        concat_axis=0,
        tiled=True,
    )
    arrived = arrived.reshape(rows_dev, feature_width)[arrange]
    listed_all = blocks.reshape(peer_count, clusters_dev * SHORT)
    owner_base = group_index * peer_count
    planner = partial(
        request_plan, owner_base=owner_base, peer_count=peer_count, per_owner=per_owner
    )
    places_all, tables_all = jax.vmap(planner)(listed_all)
    own_places = places_all[own_index].reshape(clusters_dev, SHORT)
    wanted_flat = tables_all[:, own_index, :].reshape(-1)
    block_range = jnp.arange(labels.shape[0], dtype=jnp.int32)
    reply_pick = (wanted_flat[:, None] == block_range[None, :]).astype(jnp.bfloat16)
    reply_blocks = jnp.einsum(
        "sb,bjd->sjd", reply_pick, labels, preferred_element_type=jnp.float32
    ).astype(jnp.bfloat16)
    fetched = lax.all_to_all(
        reply_blocks.reshape(peer_count, per_owner, BLK, feature_width),
        "dev",
        split_axis=0,
        concat_axis=0,
        tiled=True,
    )
    fetched = fetched.reshape(slots_total, BLK, feature_width)
    listed_ids = listed_all[own_index].reshape(clusters_dev, SHORT)
    cluster_rows = arrived.reshape(clusters_dev, CSIZE, feature_width)
    wanted_pos = positives.reshape(clusters_dev, CSIZE, NPOS)
    offsets = jnp.arange(BLK, dtype=jnp.int32)
    slot_range = jnp.arange(slots_total, dtype=jnp.int32)
    place_pick = (own_places[:, :, None] == slot_range[None, None, :]).astype(jnp.bfloat16)

    def per_cluster(running, pieces):
        rows_here, pick_here, ids_here, pos_here = pieces
        chosen = jnp.einsum(
            "ks,sjd->kjd", pick_here, fetched, preferred_element_type=jnp.float32
        ).astype(jnp.bfloat16)
        logits = jnp.einsum("qd,kjd->qkj", rows_here, chosen, preferred_element_type=jnp.float32)
        label_ids = ids_here[:, None] * BLK + offsets[None, :]
        targets = jnp.any(
            label_ids[None, :, :, None] == pos_here[:, None, None, :], axis=-1
        ).astype(jnp.float32)
        loss_rows = jnp.mean(jax.nn.softplus(logits) - targets * logits, axis=(1, 2))
        errors = (jax.nn.sigmoid(logits) - targets).astype(jnp.bfloat16)
        grad_rows = jnp.einsum(
            "qkj,kjd->qd", errors, chosen, preferred_element_type=jnp.float32
        ).astype(jnp.bfloat16)
        terms_cluster = jnp.einsum(
            "qkj,qd->kjd", errors, rows_here, preferred_element_type=jnp.float32
        )
        return (running, (loss_rows, grad_rows, terms_cluster))

    pieces = (cluster_rows, place_pick, listed_ids, wanted_pos)
    running, (losses, grads, terms) = lax.scan(per_cluster, jnp.zeros((), jnp.float32), pieces)
    selector = (own_places.reshape(-1)[:, None] == slot_range[None, :]).astype(jnp.float32)
    summed = jnp.einsum(
        "rs,rjd->sjd",
        selector,
        terms.reshape(-1, BLK, feature_width),
        precision=lax.Precision.HIGHEST,
        preferred_element_type=jnp.float32,
    )
    returned_grads = lax.all_to_all(
        summed.astype(jnp.bfloat16).reshape(peer_count, per_owner, BLK, feature_width),
        "dev",
        split_axis=0,
        concat_axis=0,
        tiled=True,
    )
    returned_grads = returned_grads.reshape(slots_total, BLK, feature_width)
    label_grad = jnp.einsum(
        "sb,sjd->bjd", reply_pick, returned_grads, preferred_element_type=jnp.float32
    ).astype(jnp.bfloat16)
    cluster_grad = grads.reshape(rows_dev, feature_width)
    returned = lax.all_to_all(
        cluster_grad[incoming].reshape(peer_count, per_peer, feature_width),
        "dev",
        split_axis=0,
        concat_axis=0,
        tiled=True,
    )
    restored = returned.reshape(rows_dev, feature_width)[jnp.argsort(outbound)]
    grad_pre = (restored.astype(jnp.float32) * activate_slope(pre_act)).astype(jnp.bfloat16)
    back_term = jnp.einsum("qe,de->qd", grad_pre, w_res, preferred_element_type=jnp.float32)
    query_grad = (restored.astype(jnp.float32) + back_term).astype(jnp.bfloat16)
    weight_term = jnp.einsum("qd,qe->de", queries, grad_pre, preferred_element_type=jnp.float32)
    weight_sum = lax.psum(weight_term, ("grp", "dev"))
    scale_factor = float(rows_dev * peer_count * groups) ** (-0.5)
    return (
        losses.reshape(rows_dev),
        query_grad,
        label_grad,
        (weight_sum * scale_factor).astype(jnp.bfloat16),
    )


def solution(mesh):
    in_specs = (
        P(("grp", "dev"), None),
        P("grp"),
        P(),
        P(("grp", "dev"), None, None),
        P("grp", None),
        P(("grp", "dev"), None),
    )
    out_specs = (P(("grp", "dev")), P(("grp", "dev"), None), P(("grp", "dev"), None, None), P())
    return jax.shard_map(local, mesh=mesh, in_specs=in_specs, out_specs=out_specs, check_vma=False)
```

profile of v0, /device:TPU:2, one launch (start us, length us, event | category | flops | bytes accessed | tf_op | source)
XLA Modules:
  0.0 643.6 jit_solution(3490546229624405968)
XLA Ops:
  7.2 0.9 and_select_fusion
  8.1 3.2 sort.65
  11.2 2.6 add_convert_fusion
  13.8 1.9 gather_fusion
  15.8 11.5 %all-to-all-start = ((bf16[32,8,768]{2,1,0:T(8,128)(2,1)}), bf16[32,8,768]{2,1,0:T(8,128)(2,1)S(1)}, u32[]{:S(2)}, u32[]{:S(2)}) async-start(bf16[32,8,768]{2,1,0:T(8,128)(2,1)} %bitcast), calls=%async_computation | async-start | bytes 786432 | tf_op jit(solution)/shard_map/all_to_all | solution.py:65
  28.9 37.8 %scatter_fusion = s32[32,32]{1,0:T(8,128)S(1)} fusion(s32[32,32]{1,0:T(8,128)S(1)} %broadcast_in_dim.65, s32[768]{0:T(1024)S(1)} %reshape.324, s32[768]{0:T(1024)S(1)} %reshape.326), kind=kCustom, calls=%fused_computation.6 | custom fusion | bytes 15360 | tf_op jit(solution)/shard_map/vmap()/scatter | solution.py:37
  66.9 5.4 convert_bitcast_fusion.1
  72.3 6.3 copy.115
  78.5 10.0 %all-to-all-start.1 = ((bf16[32,1,128,768]{3,2,1,0:T(8,128)(2,1)}), bf16[32,1,128,768]{3,2,1,0:T(8,128)(2,1)}, u32[]{:S(2)}, u32[]{:S(2)}) async-start(bf16[32,1,128,768]{3,2,1,0:T(8,128)(2,1)} %copy.115), calls=%async_computation.1 | async-start | bytes 12582912 | tf_op jit(solution)/shard_map/all_to_all | solution.py:86
  88.7 0.6 add_select_fusion
  89.3 0.6 iota.54
  90.0 1.3 compare_reduce_fusion.1
  91.4 5.3 gather_fusion.5
  97.1 0.8 fusion.43
  97.9 65.0 %gather_fusion.4 = s32[8192]{0:T(1024)S(1)} fusion(s32[32,256]{1,0:T(8,128)S(1)} %reshape.266, s32[8192]{0:T(1024)S(1)} %bitcast.111), kind=kCustom, calls=%fused_computation.4 | custom fusion | bytes 131072 | tf_op jit(solution)/shard_map/jit(take_along_axis)/gather | solution.py:57
  163.3 3.2 sort.67
  166.5 1.2 gather_fusion.1
  167.7 60.9 %all-to-all-done.1 = bf16[32,1,128,768]{3,2,1,0:T(8,128)(2,1)} async-done(((bf16[32,1,128,768]{3,2,1,0:T(8,128)(2,1)}), bf16[32,1,128,768]{3,2,1,0:T(8,128)(2,1)}, u32[]{:S(2)}, u32[]{:S(2)}) %all-to-all-start.1) | async-done | bytes 6291488 | tf_op jit(solution)/shard_map/all_to_all | solution.py:86
  228.5 9.0 %copy.116 = bf16[32,128,768]{2,0,1:T(8,128)(2,1)} copy(bf16[32,128,768]{2,1,0:T(8,128)(2,1)} %bitcast.9) | data formatting | bytes 12582912
  237.5 22.7 %while.15 = (s32[]{:T(128)}, f32[2,128]{1,0:T(2,128)S(1)}, bf16[2,128,768]{2,1,0:T(8,128)(2,1)S(1)}, f32[2,12,128,768]{3,2,1,0:T(8,128)}, bf16[2,128,768]{2,1,0:...) while((s32[]{:T(128)}, f32[2,128]{1,0:T(2,128)S(1)}, ...), condition=%wide.region_10.11_spmd.clone, body=%wide.region_7.10_spmd.clone.sunk | while | flops 988628480 | bytes 24667932 | solution.py:122
  237.6 0.5 compare_reduce_fusion.3
  238.1 0.3 copy.148
  238.4 3.8 fusion.90
  242.2 1.5 fusion.91
  243.7 1.6 fusion.92
  245.3 0.6 subtract_reduce_fusion.2
  245.9 2.9 bitcast_dynamic-update-slice_fusion.2
  248.9 0.5 compare_reduce_fusion.3
  249.4 0.3 copy.148
  249.7 3.8 fusion.90
  253.5 1.5 fusion.91
  255.0 1.6 fusion.92
  256.6 0.6 subtract_reduce_fusion.2
  257.2 2.9 bitcast_dynamic-update-slice_fusion.2
  260.2 1.9 gather_fusion.2
  262.1 8.2 %all-to-all-start.2 = ((bf16[32,8,768]{2,1,0:T(8,128)(2,1)}), bf16[32,8,768]{2,1,0:T(8,128)(2,1)S(1)}, u32[]{:S(2)}, u32[]{:S(2)}) async-start(bf16[32,8,768]{2,1,0:T(8,128)(2,1)} %bitcast.14), calls=%async_computation.2 | async-start | bytes 786432 | tf_op jit(solution)/shard_map/all_to_all | solution.py:143
  270.3 14.7 %convert_bitcast_fusion = bf16[32,1,128,768]{3,0,2,1:T(8,128)(2,1)S(1)} fusion(f32[24,128,768]{2,1,0:T(8,128)} %bitcast.115, s32[24]{0:T(128)S(1)} %get-tuple-element.171), kind=kOutput, calls=%fused_computation.42 | convolution fusion | flops 909116160 | bytes 15728736 | tf_op jit(solution)/shard_map/rs,rjd->sjd/dot_general | solution.py:124
  285.0 6.2 copy.118
  291.3 10.2 %all-to-all-start.3 = ((bf16[32,1,128,768]{3,2,1,0:T(8,128)(2,1)}), bf16[32,1,128,768]{3,2,1,0:T(8,128)(2,1)}, u32[]{:S(2)}, u32[]{:S(2)}) async-start(bf16[32,1,128,768]{3,2,1,0:T(8,128)(2,1)} %copy.118), calls=%async_computation.3 | async-start | bytes 12582912 | tf_op jit(solution)/shard_map/all_to_all | solution.py:131
  301.7 3.2 sort.68
  304.9 1.2 gather_fusion.3
  306.1 2.4 convolution_bitcast_fusion.1
  308.5 1.6 fusion.33
  310.1 312.4 %all-reduce.2.cloned.1.call-done = f32[768,768]{0,1:T(8,128)} async-done(((f32[768,768]{0,1:T(8,128)}), f32[768,768]{0,1:T(8,128)}) %all-reduce.2.cloned.1.call-update) | async-done | bytes 2359312 | tf_op jit(solution)/shard_map/psum | solution.py:155
  622.6 1.8 multiply_convert_fusion
  624.4 1.5 copy.121
  625.9 7.9 %fusion.30 = bf16[20,128,768]{2,0,1:T(8,128)(2,1)S(1)} fusion(bf16[32,1,128,768]{3,2,1,0:T(8,128)(2,1)} %all-to-all-done.3, s32[32]{0:T(128)S(1)} %dynamic-slice_reduce_fusion), kind=kOutput, calls=%fused_computation.46 | convolution fusion | flops 127795840 | bytes 10223744 | tf_op jit(solution)/shard_map/sb,sjd->bjd/dot_general | solution.py:139
  633.8 2.8 copy.120
  (88 shorter events, 3.2 us)
Async XLA Ops:
  7.2 4.1 copy-start
  7.2 20.1 %copy-start.2 = (s32[64,12]{0,1:T(8,128)S(1)}, s32[64,12]{0,1:T(8,128)}, u32[]{:S(2)}) copy-start(s32[64,12]{0,1:T(8,128)} %param.12) | copy-start | bytes 9220
  15.8 62.8 %all-to-all-start = ((bf16[32,8,768]{2,1,0:T(8,128)(2,1)}), bf16[32,8,768]{2,1,0:T(8,128)(2,1)S(1)}, u32[]{:S(2)}, u32[]{:S(2)}) async-start(bf16[32,8,768]{2,1,0:T(8,128)(2,1)} %bitcast), calls=%async_computation | async-start | bytes 786432 | tf_op jit(solution)/shard_map/all_to_all | solution.py:65
  78.5 10.1 %copy-start.3 = (s32[8192]{0:T(1024)S(1)}, s32[8192]{0:T(1024)}, u32[]{:S(2)}) copy-start(s32[8192]{0:T(1024)} %param.9) | copy-start | bytes 98308
  78.5 150.0 %all-to-all-start.1 = ((bf16[32,1,128,768]{3,2,1,0:T(8,128)(2,1)}), bf16[32,1,128,768]{3,2,1,0:T(8,128)(2,1)}, u32[]{:S(2)}, u32[]{:S(2)}) async-start(bf16[32,1,128,768]{3,2,1,0:T(8,128)(2,1)} %copy.115), calls=%async_computation.1 | async-start | bytes 12582912 | tf_op jit(solution)/shard_map/all_to_all | solution.py:86
  88.6 8.5 %sort.70.cloned.1.call-start = ((), (), s32[]{:S(2)}) async-start(), calls=%async_computation.5 | async-start | bytes 196640 | tf_op jit(solution)/shard_map/jit(argsort)/sort | solution.py:56
  97.9 65.0 %copy-start.1 = (s32[32,256]{1,0:T(8,128)S(1)}, s32[32,256]{1,0:T(8,128)}, u32[]{:S(2)}) copy-start(s32[32,256]{1,0:T(8,128)} %get-tuple-element.64) | copy-start | bytes 98308
  228.5 9.0 %copy-start.4 = (s32[256,4]{0,1:T(4,128)S(1)}, s32[256,4]{0,1:T(4,128)}, u32[]{:S(2)}) copy-start(s32[256,4]{0,1:T(4,128)} %param.13) | copy-start | bytes 12292
  260.2 24.9 %copy-start.6 = (f32[2,128]{1,0:T(2,128)}, f32[2,128]{1,0:T(2,128)S(1)}, u32[]{:S(2)}) copy-start(f32[2,128]{1,0:T(2,128)S(1)} %get-tuple-element.67) | copy-start | bytes 3076
  262.1 29.2 %all-to-all-start.2 = ((bf16[32,8,768]{2,1,0:T(8,128)(2,1)}), bf16[32,8,768]{2,1,0:T(8,128)(2,1)S(1)}, u32[]{:S(2)}, u32[]{:S(2)}) async-start(bf16[32,8,768]{2,1,0:T(8,128)(2,1)} %bitcast.14), calls=%async_computation.2 | async-start | bytes 786432 | tf_op jit(solution)/shard_map/all_to_all | solution.py:143
  291.3 14.8 %copy-start.5 = (bf16[256,768]{1,0:T(8,128)(2,1)S(1)}, bf16[256,768]{1,0:T(8,128)(2,1)}, u32[]{:S(2)}) copy-start(bf16[256,768]{1,0:T(8,128)(2,1)} %param.8) | copy-start | bytes 1179652
  291.3 14.8 %copy-start.7 = (f32[256,768]{1,0:T(8,128)S(1)}, f32[256,768]{1,0:T(8,128)}, u32[]{:S(2)}) copy-start(f32[256,768]{1,0:T(8,128)} %get-tuple-element.176) | copy-start | bytes 2359300
  291.3 334.6 %all-to-all-start.3 = ((bf16[32,1,128,768]{3,2,1,0:T(8,128)(2,1)}), bf16[32,1,128,768]{3,2,1,0:T(8,128)(2,1)}, u32[]{:S(2)}, u32[]{:S(2)}) async-start(bf16[32,1,128,768]{3,2,1,0:T(8,128)(2,1)} %copy.118), calls=%async_computation.3 | async-start | bytes 12582912 | tf_op jit(solution)/shard_map/all_to_all | solution.py:131
  301.4 321.1 %all-reduce.2.cloned.1.call-start = ((), (), s32[]{:S(2)}) async-start(), calls=%async_computation.4 | async-start | bytes 4718592 | tf_op jit(solution)/shard_map/psum | solution.py:155
Sparse Core Ops, SparseCore 0:
  92.3 2.5 sort.72.cloned.1.call-done
  308.6 313.9 all-reduce.1
  (1 shorter events, 0.0 us)
where the time goes:
time: 652 us; the launch traced here: 644 us
  waiting for transfers between devices  373 us (57%)
  local copies, waits for them, and re-layouts  143 us (22%)
  matrix products  54.2 us (8%)
  starting transfers between devices  40.1 us (6%)
  other arithmetic  17.9 us (3%)
  between operations  14.6 us (2%)
    psum x1, waiting for transfers between devices, local(): weight_sum = lax.psum(weight_term, ('grp', 'dev'))  312 us
    gather x2, local copies, waits for them, and re-layouts, local(): grid_sorted = jnp.take_along_axis(slot_grid, grid_order, axis=1)  65 us
    all_to_all x1, waiting for transfers between devices, local(): lax.all_to_all(reply_blocks.reshape(peer_count, per_owner, BLK, feature_w...  60.9 us
    scatter x3, local copies, waits for them, and re-layouts, request_plan(): jnp.full((peer_count * per_owner,), -1, jnp.int32).at[target]  38 us
    dot_general x1, matrix products, local(): jnp.einsum('rs,rjd->sjd', selector, terms.reshape(-1, BLK, feature_width)...  14.7 us
    unnamed x22, local copies, waits for them, and re-layouts  13.4 us
  transfers between devices with their start and end apart: 5, of which 2 were waited for; matrix products, arithmetic and copies ran while one was open for 25% of the time, Pallas kernels for 0%

commit v1 on v0

--- a/solution.py
+++ b/solution.py
@@ -10,6 +10,11 @@
 NPOS = 4
 POOL = 16
 BLK_DEV = 20
+
+
+def one_after_other(x, one, other):
+    partial_2 = lax.psum(x, one)
+    return lax.psum(partial_2, other)
 
 
 def activate(values):
@@ -152,7 +157,7 @@
     back_term = jnp.einsum("qe,de->qd", grad_pre, w_res, preferred_element_type=jnp.float32)
     query_grad = (restored.astype(jnp.float32) + back_term).astype(jnp.bfloat16)
     weight_term = jnp.einsum("qd,qe->de", queries, grad_pre, preferred_element_type=jnp.float32)
-    weight_sum = lax.psum(weight_term, ("grp", "dev"))
+    weight_sum = one_after_other(weight_term, "dev", "grp")
     scale_factor = float(rows_dev * peer_count * groups) ** (-0.5)
     return (
         losses.reshape(rows_dev),

time: 652 us -> 628 us (0.963)
  waiting for transfers between devices: 373 us -> 347 us
    psum x1 -> x2, waiting for transfers between devices: 312 us -> 286 us  [the longest x1 218 us: one_after_other(): partial_2 = lax.psum(x, one)]
  transfers between devices with their start and end apart: 5 -> 6, of which waited for: 2 -> 3; matrix products, arithmetic and copies ran while one was open for 25% -> 26% of each run, Pallas kernels for 0% -> 0%
where the time goes in v1:
time: 628 us; the launch traced here: 617 us
  waiting for transfers between devices  347 us (55%)
  local copies, waits for them, and re-layouts  143 us (23%)
  matrix products  54.2 us (9%)
  starting transfers between devices  40.2 us (6%)
  other arithmetic  17.9 us (3%)
  between operations  14.3 us (2%)
    psum x1, waiting for transfers between devices, one_after_other(): partial_2 = lax.psum(x, one)  218 us
    psum x1, waiting for transfers between devices, one_after_other(): return lax.psum(partial_2, other)  67.8 us
    gather x2, local copies, waits for them, and re-layouts, local(): grid_sorted = jnp.take_along_axis(slot_grid, grid_order, axis=1)  65 us
    all_to_all x1, waiting for transfers between devices, local(): lax.all_to_all(reply_blocks.reshape(peer_count, per_owner, BLK, feature_w...  60.9 us
    scatter x3, local copies, waits for them, and re-layouts, request_plan(): jnp.full((peer_count * per_owner,), -1, jnp.int32).at[target]  38 us
    dot_general x1, matrix products, local(): jnp.einsum('rs,rjd->sjd', selector, terms.reshape(-1, BLK, feature_width)...  14.7 us
    unnamed x22, local copies, waits for them, and re-layouts  13.4 us
  transfers between devices with their start and end apart: 6, of which 3 were waited for; matrix products, arithmetic and copies ran while one was open for 26% of the time, Pallas kernels for 0%

profile of v1, /device:TPU:2, one launch (start us, length us, event | category | flops | bytes accessed | tf_op | source)
XLA Modules:
  0.0 616.9 jit_solution(13595869501494977813)
XLA Ops:
  7.2 0.9 and_select_fusion
  8.1 3.2 sort.65
  11.2 2.6 add_convert_fusion
  13.8 1.9 gather_fusion
  15.8 11.5 %all-to-all-start = ((bf16[32,8,768]{2,1,0:T(8,128)(2,1)}), bf16[32,8,768]{2,1,0:T(8,128)(2,1)S(1)}, u32[]{:S(2)}, u32[]{:S(2)}) async-start(bf16[32,8,768]{2,1,0:T(8,128)(2,1)} %bitcast), calls=%async_computation | async-start | bytes 786432 | tf_op jit(solution)/shard_map/all_to_all | solution.py:70
  28.9 37.8 %scatter_fusion = s32[32,32]{1,0:T(8,128)S(1)} fusion(s32[32,32]{1,0:T(8,128)S(1)} %broadcast_in_dim.65, s32[768]{0:T(1024)S(1)} %reshape.324, s32[768]{0:T(1024)S(1)} %reshape.326), kind=kCustom, calls=%fused_computation.6 | custom fusion | bytes 15360 | tf_op jit(solution)/shard_map/vmap()/scatter | solution.py:42
  66.9 5.4 convert_bitcast_fusion.1
  72.3 6.3 %copy.115 = bf16[32,1,128,768]{3,2,1,0:T(8,128)(2,1)} copy(bf16[32,1,128,768]{3,0,2,1:T(8,128)(2,1)S(1)} %convert_bitcast_fusion.1) | data formatting | bytes 12582912 | tf_op jit(solution)/shard_map/reshape | solution.py:92
  78.5 10.0 %all-to-all-start.1 = ((bf16[32,1,128,768]{3,2,1,0:T(8,128)(2,1)}), bf16[32,1,128,768]{3,2,1,0:T(8,128)(2,1)}, u32[]{:S(2)}, u32[]{:S(2)}) async-start(bf16[32,1,128,768]{3,2,1,0:T(8,128)(2,1)} %copy.115), calls=%async_computation.1 | async-start | bytes 12582912 | tf_op jit(solution)/shard_map/all_to_all | solution.py:91
  88.7 0.6 add_select_fusion
  89.3 0.6 iota.54
  90.0 1.3 compare_reduce_fusion.1
  91.4 5.3 gather_fusion.5
  97.1 0.8 fusion.43
  97.9 65.0 %gather_fusion.4 = s32[8192]{0:T(1024)S(1)} fusion(s32[32,256]{1,0:T(8,128)S(1)} %reshape.266, s32[8192]{0:T(1024)S(1)} %bitcast.111), kind=kCustom, calls=%fused_computation.4 | custom fusion | bytes 131072 | tf_op jit(solution)/shard_map/jit(take_along_axis)/gather | solution.py:62
  163.3 3.2 sort.67
  166.5 1.2 gather_fusion.1
  167.7 60.9 %all-to-all-done.1 = bf16[32,1,128,768]{3,2,1,0:T(8,128)(2,1)} async-done(((bf16[32,1,128,768]{3,2,1,0:T(8,128)(2,1)}), bf16[32,1,128,768]{3,2,1,0:T(8,128)(2,1)}, u32[]{:S(2)}, u32[]{:S(2)}) %all-to-all-start.1) | async-done | bytes 6291488 | tf_op jit(solution)/shard_map/all_to_all | solution.py:91
  228.5 9.0 %copy.116 = bf16[32,128,768]{2,0,1:T(8,128)(2,1)} copy(bf16[32,128,768]{2,1,0:T(8,128)(2,1)} %bitcast.9) | data formatting | bytes 12582912
  237.5 22.7 %while.15 = (s32[]{:T(128)}, f32[2,128]{1,0:T(2,128)S(1)}, bf16[2,128,768]{2,1,0:T(8,128)(2,1)S(1)}, f32[2,12,128,768]{3,2,1,0:T(8,128)}, bf16[2,128,768]{2,1,0:...) while((s32[]{:T(128)}, f32[2,128]{1,0:T(2,128)S(1)}, ...), condition=%wide.region_10.11_spmd.clone, body=%wide.region_7.10_spmd.clone.sunk | while | flops 988628480 | bytes 24667932 | solution.py:127
  237.6 0.5 compare_reduce_fusion.3
  238.1 0.3 copy.148
  238.4 3.8 fusion.90
  242.2 1.5 fusion.91
  243.7 1.6 fusion.92
  245.3 0.6 subtract_reduce_fusion.2
  245.9 2.9 bitcast_dynamic-update-slice_fusion.2
  248.9 0.5 compare_reduce_fusion.3
  249.7 3.8 fusion.90
  253.5 1.5 fusion.91
  255.0 1.6 fusion.92
  256.6 0.6 subtract_reduce_fusion.2
  257.2 2.9 bitcast_dynamic-update-slice_fusion.2
  260.2 1.9 gather_fusion.2
  262.1 8.2 %all-to-all-start.2 = ((bf16[32,8,768]{2,1,0:T(8,128)(2,1)}), bf16[32,8,768]{2,1,0:T(8,128)(2,1)S(1)}, u32[]{:S(2)}, u32[]{:S(2)}) async-start(bf16[32,8,768]{2,1,0:T(8,128)(2,1)} %bitcast.14), calls=%async_computation.2 | async-start | bytes 786432 | tf_op jit(solution)/shard_map/all_to_all | solution.py:148
  270.3 14.7 %convert_bitcast_fusion = bf16[32,1,128,768]{3,0,2,1:T(8,128)(2,1)S(1)} fusion(f32[24,128,768]{2,1,0:T(8,128)} %bitcast.115, s32[24]{0:T(128)S(1)} %get-tuple-element.171), kind=kOutput, calls=%fused_computation.42 | convolution fusion | flops 909116160 | bytes 15728736 | tf_op jit(solution)/shard_map/rs,rjd->sjd/dot_general | solution.py:129
  285.0 6.2 %copy.118 = bf16[32,1,128,768]{3,2,1,0:T(8,128)(2,1)} copy(bf16[32,1,128,768]{3,0,2,1:T(8,128)(2,1)S(1)} %convert_bitcast_fusion) | data formatting | bytes 12582912 | tf_op jit(solution)/shard_map/reshape | solution.py:137
  291.3 10.2 %all-to-all-start.3 = ((bf16[32,1,128,768]{3,2,1,0:T(8,128)(2,1)}), bf16[32,1,128,768]{3,2,1,0:T(8,128)(2,1)}, u32[]{:S(2)}, u32[]{:S(2)}) async-start(bf16[32,1,128,768]{3,2,1,0:T(8,128)(2,1)} %copy.118), calls=%async_computation.3 | async-start | bytes 12582912 | tf_op jit(solution)/shard_map/all_to_all | solution.py:136
  301.7 3.2 sort.68
  304.9 1.2 gather_fusion.3
  306.1 2.4 convolution_bitcast_fusion.1
  308.5 218.2 %all-reduce.3.cloned.1.call-done = f32[768,768]{0,1:T(8,128)} async-done(((f32[768,768]{0,1:T(8,128)}), f32[768,768]{0,1:T(8,128)}) %all-reduce.3.cloned.1.call-update) | async-done | bytes 2359312 | tf_op jit(solution)/shard_map/psum | solution.py:16
  526.8 1.6 fusion.33
  528.4 67.8 %all-reduce.5.cloned.1.call-done = f32[768,768]{0,1:T(8,128)} async-done(((f32[768,768]{0,1:T(8,128)}), f32[768,768]{0,1:T(8,128)}) %all-reduce.5.cloned.1.call-update) | async-done | bytes 2359312 | tf_op jit(solution)/shard_map/psum | solution.py:17
  596.2 1.8 multiply_convert_fusion
  598.0 1.5 copy.121
  599.5 7.9 %fusion.30 = bf16[20,128,768]{2,0,1:T(8,128)(2,1)S(1)} fusion(bf16[32,1,128,768]{3,2,1,0:T(8,128)(2,1)} %all-to-all-done.3, s32[32]{0:T(128)S(1)} %dynamic-slice_reduce_fusion), kind=kOutput, calls=%fused_computation.46 | convolution fusion | flops 127795840 | bytes 10223744 | tf_op jit(solution)/shard_map/sb,sjd->bjd/dot_general | solution.py:144
  607.4 2.8 copy.120
  (91 shorter events, 3.6 us)
Async XLA Ops:
  7.2 4.1 copy-start
  7.2 20.1 %copy-start.2 = (s32[64,12]{0,1:T(8,128)S(1)}, s32[64,12]{0,1:T(8,128)}, u32[]{:S(2)}) copy-start(s32[64,12]{0,1:T(8,128)} %param.12) | copy-start | bytes 9220
  15.8 62.8 %all-to-all-start = ((bf16[32,8,768]{2,1,0:T(8,128)(2,1)}), bf16[32,8,768]{2,1,0:T(8,128)(2,1)S(1)}, u32[]{:S(2)}, u32[]{:S(2)}) async-start(bf16[32,8,768]{2,1,0:T(8,128)(2,1)} %bitcast), calls=%async_computation | async-start | bytes 786432 | tf_op jit(solution)/shard_map/all_to_all | solution.py:70
  78.5 10.1 %copy-start.3 = (s32[8192]{0:T(1024)S(1)}, s32[8192]{0:T(1024)}, u32[]{:S(2)}) copy-start(s32[8192]{0:T(1024)} %param.9) | copy-start | bytes 98308
  78.5 150.0 %all-to-all-start.1 = ((bf16[32,1,128,768]{3,2,1,0:T(8,128)(2,1)}), bf16[32,1,128,768]{3,2,1,0:T(8,128)(2,1)}, u32[]{:S(2)}, u32[]{:S(2)}) async-start(bf16[32,1,128,768]{3,2,1,0:T(8,128)(2,1)} %copy.115), calls=%async_computation.1 | async-start | bytes 12582912 | tf_op jit(solution)/shard_map/all_to_all | solution.py:91
  88.6 8.5 %sort.70.cloned.1.call-start = ((), (), s32[]{:S(2)}) async-start(), calls=%async_computation.6 | async-start | bytes 196640 | tf_op jit(solution)/shard_map/jit(argsort)/sort | solution.py:61
  97.9 65.0 %copy-start.1 = (s32[32,256]{1,0:T(8,128)S(1)}, s32[32,256]{1,0:T(8,128)}, u32[]{:S(2)}) copy-start(s32[32,256]{1,0:T(8,128)} %get-tuple-element.64) | copy-start | bytes 98308
  228.5 9.0 %copy-start.4 = (s32[256,4]{0,1:T(4,128)S(1)}, s32[256,4]{0,1:T(4,128)}, u32[]{:S(2)}) copy-start(s32[256,4]{0,1:T(4,128)} %param.13) | copy-start | bytes 12292
  260.2 24.9 %copy-start.6 = (f32[2,128]{1,0:T(2,128)}, f32[2,128]{1,0:T(2,128)S(1)}, u32[]{:S(2)}) copy-start(f32[2,128]{1,0:T(2,128)S(1)} %get-tuple-element.67) | copy-start | bytes 3076
  262.1 29.2 %all-to-all-start.2 = ((bf16[32,8,768]{2,1,0:T(8,128)(2,1)}), bf16[32,8,768]{2,1,0:T(8,128)(2,1)S(1)}, u32[]{:S(2)}, u32[]{:S(2)}) async-start(bf16[32,8,768]{2,1,0:T(8,128)(2,1)} %bitcast.14), calls=%async_computation.2 | async-start | bytes 786432 | tf_op jit(solution)/shard_map/all_to_all | solution.py:148
  291.3 14.8 %copy-start.5 = (bf16[256,768]{1,0:T(8,128)(2,1)S(1)}, bf16[256,768]{1,0:T(8,128)(2,1)}, u32[]{:S(2)}) copy-start(bf16[256,768]{1,0:T(8,128)(2,1)} %param.8) | copy-start | bytes 1179652
  291.3 14.8 %copy-start.7 = (f32[256,768]{1,0:T(8,128)S(1)}, f32[256,768]{1,0:T(8,128)}, u32[]{:S(2)}) copy-start(f32[256,768]{1,0:T(8,128)} %get-tuple-element.176) | copy-start | bytes 2359300
  291.3 308.2 %all-to-all-start.3 = ((bf16[32,1,128,768]{3,2,1,0:T(8,128)(2,1)}), bf16[32,1,128,768]{3,2,1,0:T(8,128)(2,1)}, u32[]{:S(2)}, u32[]{:S(2)}) async-start(bf16[32,1,128,768]{3,2,1,0:T(8,128)(2,1)} %copy.118), calls=%async_computation.3 | async-start | bytes 12582912 | tf_op jit(solution)/shard_map/all_to_all | solution.py:136
  301.4 225.3 %all-reduce.3.cloned.1.call-start = ((), (), s32[]{:S(2)}) async-start(), calls=%async_computation.4 | async-start | bytes 4718592 | tf_op jit(solution)/shard_map/psum | solution.py:16
  308.5 287.7 %all-reduce.5.cloned.1.call-start = ((), (), s32[]{:S(2)}) async-start(), calls=%async_computation.5 | async-start | bytes 4718592 | tf_op jit(solution)/shard_map/psum | solution.py:17
Sparse Core Ops, SparseCore 0:
  92.3 2.5 sort.72.cloned.1.call-done
  308.6 218.1 all-reduce.2
  529.2 66.9 all-reduce.4
  (1 shorter events, 0.0 us)
